TPU v7x, 32 devices: a whole 2x2x4 slice. The times are simulated.
32 devices in a mesh: req: 8 (over z, x), mlp: 4 (over y, core).
Axes of the slice: x: 2, y: 2, z: 4, core: 2. Of those that a mesh axis runs over, the one named last changes fastest.
Arguments:
- tokens: bfloat16 [8192, 2048], P('req', 'mlp'), may hold values from -40 to 40, as said below
- norm_gain_vector: bfloat16 [2048], replicated, may hold values from 0.099609375 to 1.8984375
- gate_weight: bfloat16 [2048, 3584], P(None, 'mlp'), may hold values from -0.125 to 0.125
- up_weight: bfloat16 [2048, 3584], P(None, 'mlp'), may hold values from -0.125 to 0.125
- down_weight: bfloat16 [3584, 2048], P('mlp'), may hold values from -0.09375 to 0.09375
- gate_up_input_maps: bfloat16 [8, 2048, 32], P('req'), may hold values from -0.125 to 0.125
- gate_up_output_maps: bfloat16 [8, 2, 16, 3584], P('req', None, None, 'mlp'), may hold values from -1.5 to 1.5
- down_input_maps: bfloat16 [8, 3584, 16], P('req', 'mlp'), may hold values from -0.09375 to 0.09375
- down_output_maps: bfloat16 [8, 16, 2048], P('req'), may hold values from -1.5 to 1.5
- lengths: int32 [8, 4], replicated, may hold values from 0 to 1024, as said below
- request_adapter_slot: int32 [8, 4], replicated, may hold values from 0 to 7
- selected: int32 [8], replicated, may hold values from 0 to 7, as said below
Outputs:
- layer_out: bfloat16 [8192, 2048], P('req', 'mlp')
Inputs may be any that keep to these rules, and one draw needn't show every extreme that they name: Each row of lengths sums to a multiple of 64 from 64 to 1024; some row sums to exactly 1024 and holds all of it in one slot; all rows together sum to 4096. Slots may hold zero tokens. `selected`: 8 different adapter ids; adapter a is owned by index a // 1 of req. `tokens`: entries of order one, some rows and features larger than others.
All inputs are finite; a program needn't handle non-finite values.
Results may differ from a plain program's by a relative error of at most 0.006.
Values may be sent and summed in bfloat16 or wider, within the bound.
A program may use at most 128 MiB of HBM per device.

v0:
```python
import jax
import jax.numpy as jnp
from jax import lax
from jax.sharding import PartitionSpec as P

TOK_DEV = 512
EPSILON = 1e-06


def gather_adapter_maps(gate_up_input_maps, gate_up_output_maps, down_input_maps, down_output_maps):
    token_count = gate_up_input_maps.shape[0]
    return jnp.concatenate(
        [
            gate_up_input_maps.reshape(token_count, -1),
            gate_up_output_maps.reshape(token_count, -1),
            down_input_maps.reshape(token_count, -1),
            down_output_maps.reshape(token_count, -1),
        ],
        axis=1,
    )


def unpack_adapters(packed_adapters, width_size, rank_size, inner_hidden):
    token_count = packed_adapters.shape[0]
    first_branch = width_size * 2 * rank_size
    second_branch = first_branch + 2 * rank_size * inner_hidden
    third = second_branch + inner_hidden * rank_size
    gate_up_input_maps = packed_adapters[:, :first_branch].reshape(
        token_count, width_size, 2 * rank_size
    )
    gate_up_output_maps = packed_adapters[:, first_branch:second_branch].reshape(
        token_count, 2, rank_size, inner_hidden
    )
    down_input_maps = packed_adapters[:, second_branch:third].reshape(
        token_count, inner_hidden, rank_size
    )
    down_output_maps = packed_adapters[:, third:].reshape(token_count, rank_size, width_size)
    return (gate_up_input_maps, gate_up_output_maps, down_input_maps, down_output_maps)


def slot_table(owners, positions, lengths, request_adapter_slot, token_count):
    lens = jnp.take(lengths, owners, axis=0)
    req_ends = jnp.cumsum(lens, axis=1)
    starts = req_ends - lens
    inside = (positions[:, None] >= starts) & (positions[:, None] < req_ends)
    adapter_ids = jnp.take(request_adapter_slot, owners, axis=0)
    picked = jnp.sum(jnp.where(inside, adapter_ids, 0), axis=1)
    live = jnp.any(inside, axis=1)
    onehot = (picked[:, None] == jnp.arange(token_count, dtype=jnp.int32)[None, :]) & live[:, None]
    return onehot.astype(jnp.float32)


def mlp_partial(
    whole, norm_gain_vector, gate_weight, up_weight, down_weight, adapter_table, onehot
):
    gate_up_input_maps, gate_up_output_maps, down_input_maps, down_output_maps = adapter_table
    rank_size = down_output_maps.shape[1]
    values = whole.astype(jnp.float32)
    mean_square = jnp.mean(values * values, axis=1, keepdims=True)
    normed_input = (
        values * lax.rsqrt(mean_square + EPSILON) * norm_gain_vector.astype(jnp.float32)
    ).astype(jnp.bfloat16)
    low_rank_term = jnp.einsum(
        "ec,mch->emh", normed_input, gate_up_input_maps, preferred_element_type=jnp.float32
    )
    low_rank_term = (low_rank_term * onehot[:, :, None]).astype(jnp.bfloat16)
    gate_sum = jnp.dot(normed_input, gate_weight, preferred_element_type=jnp.float32) + jnp.einsum(
        "vca,can->vn",
        low_rank_term[:, :, :rank_size],
        gate_up_output_maps[:, 0],
        preferred_element_type=jnp.float32,
    )
    up_sum = jnp.dot(normed_input, up_weight, preferred_element_type=jnp.float32) + jnp.einsum(
        "vca,can->vn",
        low_rank_term[:, :, rank_size:],
        gate_up_output_maps[:, 1],
        preferred_element_type=jnp.float32,
    )
    hidden = (jax.nn.silu(gate_sum) * up_sum).astype(jnp.bfloat16)
    down_rank = (
        jnp.einsum("tf,sfr->tsr", hidden, down_input_maps, preferred_element_type=jnp.float32)
        * onehot[:, :, None]
    )
    down_term = jnp.einsum(
        "tsr,srd->td",
        down_rank,
        down_output_maps.astype(jnp.float32),
        precision=lax.Precision.HIGHEST,
        preferred_element_type=jnp.float32,
    )
    return jnp.dot(hidden, down_weight, preferred_element_type=jnp.float32) + down_term


def on_device(
    tokens,
    norm_gain_vector,
    gate_weight,
    up_weight,
    down_weight,
    gate_up_input_maps,
    gate_up_output_maps,
    down_input_maps,
    down_output_maps,
    lengths,
    request_adapter_slot,
    selected,
):
    groups = lax.axis_size("req")
    device = lax.axis_index("req")
    capacity, columns = tokens.shape
    chosen_count = selected.shape[0]
    rank_size = down_output_maps.shape[1]
    width_size = down_output_maps.shape[2]
    inner_hidden = down_input_maps.shape[1]
    packed_adapters = gather_adapter_maps(
        gate_up_input_maps, gate_up_output_maps, down_input_maps, down_output_maps
    )
    every = lax.all_gather(packed_adapters, "req", axis=0, tiled=True)
    chosen = jnp.take(every, selected, axis=0)
    adapter_table = unpack_adapters(chosen, width_size, rank_size, inner_hidden)
    totals = jnp.sum(lengths, axis=1)
    block_rows = TOK_DEV // groups
    spread = capacity // TOK_DEV
    counts = totals // block_rows
    group_ends = jnp.cumsum(counts)
    offsets = group_ends - counts
    turn_by = offsets[device] % groups
    blocks = tokens.reshape(spread, groups, block_rows, columns)
    outgoing = jnp.roll(blocks, turn_by, axis=1)
    incoming = lax.all_to_all(outgoing, "req", split_axis=1, concat_axis=1, tiled=True)
    places = jnp.arange(groups, dtype=jnp.int32)
    global_ids = places * groups + device
    owners = jnp.sum((group_ends[None, :] <= global_ids[:, None]).astype(jnp.int32), axis=1)
    inner_ids = global_ids - jnp.take(offsets, owners)
    indices = inner_ids // groups * groups + owners
    flat_blocks = incoming.reshape(spread * groups, block_rows, columns)
    balanced = jnp.take(flat_blocks, indices, axis=0).reshape(groups * block_rows, columns)
    row_owner = jnp.repeat(owners, block_rows)
    row_position = (
        inner_ids[:, None] * block_rows + jnp.arange(block_rows, dtype=jnp.int32)[None, :]
    ).reshape(-1)
    onehot = slot_table(row_owner, row_position, lengths, request_adapter_slot, chosen_count)
    whole = lax.all_gather(balanced, "mlp", axis=1, tiled=True)
    partial_value = mlp_partial(
        whole, norm_gain_vector, gate_weight, up_weight, down_weight, adapter_table, onehot
    )
    branch = lax.psum_scatter(
        partial_value.astype(jnp.bfloat16), "mlp", scatter_dimension=1, tiled=True
    )
    back = (
        jnp.zeros((spread * groups, block_rows, columns), jnp.bfloat16)
        .at[indices]
        .set(branch.reshape(groups, block_rows, columns))
    )
    returned = lax.all_to_all(
        back.reshape(spread, groups, block_rows, columns),
        "req",
        split_axis=1,
        concat_axis=1,
        tiled=True,
    )
    branch_rows = jnp.roll(returned, -turn_by, axis=1).reshape(capacity, columns)
    branch_rows = lax.optimization_barrier(branch_rows).astype(jnp.float32)
    row_valid = jnp.arange(capacity, dtype=jnp.int32) < totals[device]
    values = tokens.astype(jnp.float32)
    return jnp.where(row_valid[:, None], values + branch_rows, values).astype(jnp.bfloat16)


def solution(mesh):
    in_specs = (
        P("req", "mlp"),
        P(),
        P(None, "mlp"),
        P(None, "mlp"),
        P("mlp", None),
        P("req", None, None),
        P("req", None, None, "mlp"),
        P("req", "mlp", None),
        P("req", None, None),
        P(),
        P(),
        P(),
    )
    out_specs = P("req", "mlp")
    return jax.shard_map(
        on_device, mesh=mesh, in_specs=in_specs, out_specs=out_specs, check_vma=False
    )
```

profile of v0, /device:TPU:0, one launch (start us, length us, event | category | flops | bytes accessed | tf_op | source)
XLA Modules:
  0.0 234.6 jit_solution(14905129458668095679)
XLA Ops:
  6.5 1.3 copy.45
  7.8 0.3 reshape.318
  8.1 0.9 copy.46
  9.2 0.9 copy.62
  10.3 7.0 %maximum_bitcast_fusion = bf16[1,1,141312]{2,1,0:T(2,128)(2,1)} fusion(bf16[1,32768]{1,0:T(2,128)(2,1)S(1)} %bitcast.101, bf16[1,14336]{1,0:T(2,128)(2,1)S(1)} %reshape.320, bf16[1,28672]{1,0:T(2,128)(2,1)S(1)} %bitcast.104, bf16[1,65536]{1,0:T(2,128)(2,1)S(1)} %reshape.318), kind=kLoop, calls=%fused_computation.28 | loop fusion | flops 1130496 | bytes 565248
  17.6 0.6 dynamic_slice.10
  20.1 0.4 fusion.8
  20.6 1.0 copy.43
  21.6 7.3 %all-to-all-start = ((bf16[2,8,64,512]{3,2,0,1:T(8,128)(2,1)}), bf16[2,8,64,512]{3,2,0,1:T(8,128)(2,1)S(1)}, u32[]{:S(2)}, u32[]{:S(2)}) async-start(bf16[2,8,64,512]{3,2,0,1:T(8,128)(2,1)} %copy.43), calls=%async_computation | async-start | bytes 2097152 | tf_op jit(solution)/shard_map/all_to_all | solution.py:130
  29.2 0.6 gather_fusion
  30.4 1.0 gather_fusion.4
  31.9 1.0 gather_fusion.5
  33.0 0.3 fusion.31
  33.3 0.2 fusion.11
  33.5 39.2 %all-to-all-done = bf16[2,8,64,512]{3,2,0,1:T(8,128)(2,1)S(1)} async-done(((bf16[2,8,64,512]{3,2,0,1:T(8,128)(2,1)}), bf16[2,8,64,512]{3,2,0,1:T(8,128)(2,1)S(1)}, u32[]{:S(2)}, u32[]{:S(2)}) %all-to-all-start) | async-done | bytes 1048608 | tf_op jit(solution)/shard_map/all_to_all | solution.py:130
  72.8 0.6 gather_fusion.1
  73.4 1.0 bitcast_select_fusion
  74.4 0.2 reduce-scatter.2.cloned.1.call-start
  74.7 43.2 %all-gather.6.cloned.1.call-done = bf16[8,1,141312]{2,1,0:T(2,128)(2,1)} async-done(((bf16[1,1,141312]{2,1,0:T(2,128)(2,1)}), bf16[8,1,141312]{2,1,0:T(2,128)(2,1)}) %all-gather.6.cloned.1.call-update) | async-done | bytes 2261008 | tf_op jit(solution)/shard_map/all_gather | solution.py:118
  117.9 3.4 %copy.70 = bf16[8,1,141312]{2,0,1:T(8,128)(2,1)S(1)} copy(bf16[8,1,141312]{2,1,0:T(2,128)(2,1)} %all-gather.6.cloned.1.call-done) | data formatting | bytes 4521984
  121.5 1.3 gather_fusion.2
  122.8 2.3 gather_fusion.3
  125.1 4.4 %maximum_select_fusion = bf16[8,141312]{1,0:T(8,128)(2,1)S(1)} fusion(bf16[8,70656]{1,0:T(8,128)(2,1)} %gather_fusion.3, bf16[8,70656]{1,0:T(8,128)(2,1)S(1)} %gather_fusion.2, pred[8]{0:T(512)(128)(4,1)S(1)} %get-tuple-element.13), kind=kLoop, calls=%fused_computation.15 | loop fusion | flops 5652480 | bytes 4521992 | tf_op jit(solution)/shard_map/jit(_take)/select_n | solution.py:119
  129.6 1.3 copy-done
  130.9 5.0 %reshape.322 = bf16[8,2048,32]{2,1,0:T(8,128)(2,1)} reshape(bf16[8,65536]{1,0:T(8,128)(2,1)S(1)} %slice.44) | data formatting | bytes 2097152 | tf_op jit(solution)/shard_map/reshape | solution.py:28
  136.0 4.6 %copy.47 = bf16[8,2048,32]{1,2,0:T(8,128)(2,1)} copy(bf16[8,2048,32]{2,1,0:T(8,128)(2,1)} %reshape.322) | data formatting | bytes 2097152 | tf_op jit(solution)/shard_map/reshape | solution.py:28
  140.7 1.5 reshape.325
  142.1 0.9 copy.52
  143.1 2.2 fusion
  145.4 2.1 fusion.27
  147.5 0.4 fusion.14
  147.9 1.6 copy-done.9
  149.5 2.4 %fusion.29 = f32[512,896]{1,0:T(8,128)S(1)} fusion(bf16[2048,896]{1,0:T(8,128)(2,1)S(1)} %copy-done.9, bf16[512,2048]{1,0:T(8,128)(2,1)S(1)} %copy-done.3, f32[2048]{0:T(1024)S(1)} %convert_element_type.41, f32[512]{0:T(512)S(1)} %add_rsqrt_fusion), kind=kOutput, calls=%fused_computation.94 | convolution fusion | flops 1883242496 | bytes 7612416 | tf_op jit(solution)/shard_map/dot_general | solution.py:67
  151.9 2.4 %fusion.25 = f32[512,896]{1,0:T(8,128)S(1)} fusion(bf16[2048,896]{1,0:T(8,128)(2,1)S(1)} %copy-done.10, bf16[512,2048]{1,0:T(8,128)(2,1)S(1)} %copy-done.3, f32[2048]{0:T(1024)S(1)} %convert_element_type.41, f32[512]{0:T(512)S(1)} %add_rsqrt_fusion), kind=kOutput, calls=%fused_computation.92 | convolution fusion | flops 1883242496 | bytes 7612416 | tf_op jit(solution)/shard_map/dot_general | solution.py:73
  154.3 0.8 fusion.6
  155.1 0.4 fusion.36
  155.6 0.8 copy-done.11
  156.4 2.3 fusion.35
  158.7 3.5 %fusion.3 = bf16[512,2048]{1,0:T(8,128)(2,1)} fusion(f32[512,2048]{1,0:T(8,128)S(1)} %fusion.35, bf16[1,8,16,2048]{3,1,2,0:T(8,128)(2,1)S(1)} %bitcast.93, f32[512,8,16]{0,2,1:T(8,128)S(1)} %bitcast.107, f32[512,8]{0,1:T(8,128)S(1)} %fusion.19), kind=kOutput, calls=%fused_computation.13 | convolution fusion | flops 1612775424 | bytes 7094272 | tf_op jit(solution)/shard_map/tsr,srd->td/dot_general | solution.py:84
  162.2 29.7 %reduce-scatter.2.cloned.1.call-done = bf16[512,512]{1,0:T(8,128)(2,1)} async-done(((bf16[512,2048]{1,0:T(8,128)(2,1)}), bf16[512,512]{1,0:T(8,128)(2,1)}) %reduce-scatter.2.cloned.1.call-update) | async-done | bytes 524304 | tf_op jit(solution)/shard_map/reduce_scatter | solution.py:147
  192.0 1.8 scatter_fusion
  193.8 1.1 copy.53
  194.9 5.5 %all-to-all-start.1 = ((bf16[2,8,64,512]{3,2,0,1:T(8,128)(2,1)}), bf16[2,8,64,512]{3,2,0,1:T(8,128)(2,1)S(1)}, u32[]{:S(2)}, u32[]{:S(2)}) async-start(bf16[2,8,64,512]{3,2,0,1:T(8,128)(2,1)} %copy.53), calls=%async_computation.2 | async-start | bytes 2097152 | tf_op jit(solution)/shard_map/all_to_all | solution.py:155
  200.4 0.6 dynamic_slice.9
  201.0 0.6 iota_compare_fusion.1
  201.7 24.5 %all-to-all-done.1 = bf16[2,8,64,512]{3,2,0,1:T(8,128)(2,1)S(1)} async-done(((bf16[2,8,64,512]{3,2,0,1:T(8,128)(2,1)}), bf16[2,8,64,512]{3,2,0,1:T(8,128)(2,1)S(1)}, u32[]{:S(2)}, u32[]{:S(2)}) %all-to-all-start.1) | async-done | bytes 1048608 | tf_op jit(solution)/shard_map/all_to_all | solution.py:155
  226.2 0.4 fusion.7
  226.7 1.4 fusion.4
  (72 shorter events, 2.5 us)
Async XLA Ops:
  6.5 3.7 %copy-start.4 = (bf16[1,2,16,896]{3,2,1,0:T(8,128)(2,1)S(1)}, bf16[1,2,16,896]{3,2,1,0:T(8,128)(2,1)}, u32[]{:S(2)}) copy-start(bf16[1,2,16,896]{3,2,1,0:T(8,128)(2,1)} %param.22) | copy-start | bytes 172036
  6.5 10.8 %copy-start.5 = (s32[8,4]{0,1:T(4,128)S(1)}, s32[8,4]{0,1:T(4,128)}, u32[]{:S(2)}) copy-start(s32[8,4]{0,1:T(4,128)} %param.25) | copy-start | bytes 388
  6.5 13.6 %copy-start.1 = (bf16[1024,512]{1,0:T(8,128)(2,1)S(1)}, bf16[1024,512]{1,0:T(8,128)(2,1)}, u32[]{:S(2)}) copy-start(bf16[1024,512]{1,0:T(8,128)(2,1)} %param.16) | copy-start | bytes 3145732
  6.5 111.3 %all-gather.6.cloned.1.call-start = ((), (), s32[]{:S(2)}) async-start(), calls=%async_computation.5 | async-start | bytes 5087232 | tf_op jit(solution)/shard_map/all_gather | solution.py:118
  20.5 9.3 %copy-start.8 = (s32[8]{0:T(128)S(1)}, s32[8]{0:T(128)}, u32[]{:S(2)}) copy-start(s32[8]{0:T(128)} %param.27) | copy-start | bytes 100
  20.5 9.5 %copy-start.6 = (bf16[2048]{0:T(1024)(128)(2,1)S(1)}, bf16[2048]{0:T(1024)(128)(2,1)}, u32[]{:S(2)}) copy-start(bf16[2048]{0:T(1024)(128)(2,1)} %param.17) | copy-start | bytes 12292
  21.6 51.1 %all-to-all-start = ((bf16[2,8,64,512]{3,2,0,1:T(8,128)(2,1)}), bf16[2,8,64,512]{3,2,0,1:T(8,128)(2,1)S(1)}, u32[]{:S(2)}, u32[]{:S(2)}) async-start(bf16[2,8,64,512]{3,2,0,1:T(8,128)(2,1)} %copy.43), calls=%async_computation | async-start | bytes 2097152 | tf_op jit(solution)/shard_map/all_to_all | solution.py:130
  28.8 2.9 %copy-start.7 = (s32[8,4]{0,1:T(4,128)S(1)}, s32[8,4]{0,1:T(4,128)}, u32[]{:S(2)}) copy-start(s32[8,4]{0,1:T(4,128)} %param.26) | copy-start | bytes 388
  28.8 114.3 %all-gather.4.cloned.1.call-start = ((), (), s32[]{:S(2)}) async-start(), calls=%async_computation.3 | async-start | bytes 2621440 | tf_op jit(solution)/shard_map/all_gather | solution.py:143
  74.4 117.5 %reduce-scatter.2.cloned.1.call-start = ((), (), s32[]{:S(2)}) async-start(), calls=%async_computation.4 | async-start | bytes 2621440 | tf_op jit(solution)/shard_map/reduce_scatter | solution.py:147
  129.5 1.4 copy-start
  136.0 4.6 %slice-start = ((bf16[8,141312]{1,0:T(8,128)(2,1)}), bf16[8,28672]{1,0:T(8,128)(2,1)S(1)}, s32[]{:S(2)}) async-start(bf16[8,141312]{1,0:T(8,128)(2,1)} %copy-done), calls=%async_computation.6 | async-start | bytes 917504 | tf_op jit(solution)/shard_map/slice | solution.py:31
  136.0 4.7 %slice-start.1 = ((bf16[8,141312]{1,0:T(8,128)(2,1)}), bf16[8,14336]{1,0:T(8,128)(2,1)S(1)}, s32[]{:S(2)}) async-start(bf16[8,141312]{1,0:T(8,128)(2,1)} %copy-done), calls=%async_computation.7 | async-start | bytes 458752 | tf_op jit(solution)/shard_map/slice | solution.py:34
  143.1 2.2 copy-start.3
  147.5 2.0 copy-start.9
  149.5 2.4 %copy-start.10 = (bf16[2048,896]{1,0:T(8,128)(2,1)S(1)}, bf16[2048,896]{1,0:T(8,128)(2,1)}, u32[]{:S(2)}) copy-start(bf16[2048,896]{1,0:T(8,128)(2,1)} %param.19) | copy-start | bytes 11010052
  154.3 2.0 copy-start.11
  156.4 2.3 slice-start.2
  194.9 31.3 %all-to-all-start.1 = ((bf16[2,8,64,512]{3,2,0,1:T(8,128)(2,1)}), bf16[2,8,64,512]{3,2,0,1:T(8,128)(2,1)S(1)}, u32[]{:S(2)}, u32[]{:S(2)}) async-start(bf16[2,8,64,512]{3,2,0,1:T(8,128)(2,1)} %copy.53), calls=%async_computation.2 | async-start | bytes 2097152 | tf_op jit(solution)/shard_map/all_to_all | solution.py:155
  201.7 25.0 %copy-start.2 = (bf16[1024,512]{1,0:T(8,128)(2,1)S(1)}, bf16[1024,512]{1,0:T(8,128)(2,1)}, u32[]{:S(2)}) copy-start(bf16[1024,512]{1,0:T(8,128)(2,1)} %param.16) | copy-start | bytes 3145732
Sparse Core Ops, SparseCore 0:
  17.4 100.3 all-gather.5
  119.4 20.7 all-gather.3
  162.3 29.5 reduce-scatter.1
where the time goes:
time: 235 us
  waiting for transfers between devices  137 us (58%)
  local copies, waits for them, and re-layouts  36.1 us (15%)
  other arithmetic  19 us (8%)
  between operations  15.5 us (7%)
  matrix products  14.2 us (6%)
  starting transfers between devices  13 us (6%)
    all_gather x1, waiting for transfers between devices, on_device(): every = lax.all_gather(packed_adapters, 'req', axis=0, tiled=True)  43.2 us
    all_to_all x1, waiting for transfers between devices, on_device(): lax.all_to_all(outgoing, 'req', split_axis=1, concat_axis=1, tiled=True)  39.2 us
    reduce_scatter x1, waiting for transfers between devices, on_device(): lax.psum_scatter(partial_value.astype(jnp.bfloat16), 'mlp', scatter_dimen...  29.7 us
    all_to_all x1, waiting for transfers between devices, on_device(): lax.all_to_all(back.reshape(spread, groups, block_rows, columns), 'req',...  24.5 us
    unnamed x33, local copies, waits for them, and re-layouts  10.7 us
    reshape x2, local copies, waits for them, and re-layouts, unpack_adapters(): packed_adapters[:, :first_branch]  9.65 us
    all_to_all x1, starting transfers between devices, on_device(): lax.all_to_all(outgoing, 'req', split_axis=1, concat_axis=1, tiled=True)  7.25 us
    unnamed x1, other arithmetic  6.99 us
  transfers between devices with their start and end apart: 5, of which 4 were waited for; matrix products, arithmetic and copies ran while one was open for 14% of the time, Pallas kernels for 0%

commit v1 on v0

--- a/solution.py
+++ b/solution.py
@@ -5,6 +5,22 @@
 
 TOK_DEV = 512
 EPSILON = 1e-06
+
+
+def collect(x, axis, dim):
+    ways, here, step = (lax.axis_size(axis), lax.axis_index(axis), x.shape[dim])
+    lengths = [n * ways if d == dim else n for d, n in enumerate(x.shape)]
+    full = lax.dynamic_update_slice_in_dim(jnp.zeros(lengths, x.dtype), x, here * step, axis=dim)
+    going_up = going_down = x
+    for far in range(1, ways // 2 + 1):
+        going_up = lax.ppermute(going_up, axis, [(d, (d + 1) % ways) for d in range(ways)])
+        full = lax.dynamic_update_slice_in_dim(full, going_up, (here - far) % ways * step, axis=dim)
+        if 2 * far < ways:
+            going_down = lax.ppermute(going_down, axis, [(d, (d - 1) % ways) for d in range(ways)])
+            full = lax.dynamic_update_slice_in_dim(
+                full, going_down, (here + far) % ways * step, axis=dim
+            )
+    return full
 
 
 def gather_adapter_maps(gate_up_input_maps, gate_up_output_maps, down_input_maps, down_output_maps):
@@ -115,7 +131,7 @@
     packed_adapters = gather_adapter_maps(
         gate_up_input_maps, gate_up_output_maps, down_input_maps, down_output_maps
     )
-    every = lax.all_gather(packed_adapters, "req", axis=0, tiled=True)
+    every = collect(packed_adapters, "req", 0)
     chosen = jnp.take(every, selected, axis=0)
     adapter_table = unpack_adapters(chosen, width_size, rank_size, inner_hidden)
     totals = jnp.sum(lengths, axis=1)

time: 235 us -> 300 us (1.28)
  local copies, waits for them, and re-layouts: 36.1 us -> 127 us
  waiting for transfers between devices: 137 us -> 103 us
  starting transfers between devices: 13 us -> 24.2 us
  other arithmetic: 19 us -> 12.1 us
    dynamic_update_slice x0 -> x8, local copies, waits for them, and re-layouts: none -> 90.4 us  [the longest x4 45.2 us: collect(): lax.dynamic_update_slice_in_dim(full, going_up, (here - far) % ways * ste...]
    all_gather x1 -> x0, waiting for transfers between devices: 43.2 us -> none  [on_device(): every = lax.all_gather(packed_adapters, 'req', axis=0, tiled=True)]
    ppermute x0 -> x7, waiting for transfers between devices: none -> 41.3 us  [the longest x4 29.4 us: collect(): lax.ppermute(going_up, axis, [(d, (d + 1) % ways) for d in range(ways)])]
    all_to_all x1, waiting for transfers between devices: 39.2 us -> 0.01 us  [on_device(): lax.all_to_all(outgoing, 'req', split_axis=1, concat_axis=1, tiled=True)]
    ppermute x0 -> x7, starting transfers between devices: none -> 14.2 us  [the longest x4 7.96 us: collect(): lax.ppermute(going_up, axis, [(d, (d + 1) % ways) for d in range(ways)])]
    unnamed x1 -> x0, other arithmetic: 6.99 us -> none
    all_gather x1, waiting for transfers between devices: 0.02 us -> 5.88 us  [on_device(): whole = lax.all_gather(balanced, 'mlp', axis=1, tiled=True)]
    unnamed x33 -> x37, local copies, waits for them, and re-layouts: 10.7 us -> 7.03 us
  transfers between devices with their start and end apart: 5 -> 11, of which waited for: 4 -> 6; matrix products, arithmetic and copies ran while one was open for 14% -> 41% of each run, Pallas kernels for 0% -> 0%
where the time goes in v1:
time: 300 us; the launch traced here: 297 us
  local copies, waits for them, and re-layouts  127 us (42%)
  waiting for transfers between devices  103 us (34%)
  starting transfers between devices  24.2 us (8%)
  between operations  16 us (5%)
  matrix products  14.2 us (5%)
  other arithmetic  12.1 us (4%)
    dynamic_update_slice x4, local copies, waits for them, and re-layouts, collect(): lax.dynamic_update_slice_in_dim(full, going_up, (here - far) % ways * ste...  45.2 us
    dynamic_update_slice x3, local copies, waits for them, and re-layouts, collect(): lax.dynamic_update_slice_in_dim(full, going_down, (here + far) % ways * s...  33.9 us
    reduce_scatter x1, waiting for transfers between devices, on_device(): lax.psum_scatter(partial_value.astype(jnp.bfloat16), 'mlp', scatter_dimen...  31.6 us
    ppermute x4, waiting for transfers between devices, collect(): lax.ppermute(going_up, axis, [(d, (d + 1) % ways) for d in range(ways)])  29.4 us
    all_to_all x1, waiting for transfers between devices, on_device(): lax.all_to_all(back.reshape(spread, groups, block_rows, columns), 'req',...  24.5 us
    ppermute x3, waiting for transfers between devices, collect(): lax.ppermute(going_down, axis, [(d, (d - 1) % ways) for d in range(ways)])  11.9 us
    dynamic_update_slice x1, local copies, waits for them, and re-layouts, collect(): lax.dynamic_update_slice_in_dim(jnp.zeros(lengths, x.dtype), x, here * st...  11.3 us
    reshape x2, local copies, waits for them, and re-layouts, unpack_adapters(): packed_adapters[:, :first_branch]  9.66 us
  transfers between devices with their start and end apart: 11, of which 6 were waited for; matrix products, arithmetic and copies ran while one was open for 41% of the time, Pallas kernels for 0%

profile of v1, /device:TPU:0, one launch (start us, length us, event | category | flops | bytes accessed | tf_op | source)
XLA Modules:
  0.0 297.0 jit_solution(14311954195241612336)
XLA Ops:
  6.5 1.3 copy.47
  8.4 0.9 copy.62
  10.2 3.0 %collective-permute-start = (bf16[1,141312]{1,0:T(2,128)(2,1)S(1)}, bf16[1,141312]{1,0:T(2,128)(2,1)S(1)}, u32[]{:S(2)}, u32[]{:S(2)}) collective-permute-start(bf16[1,141312]{1,0:T(2,128)(2,1)S(1)} %constant_dynamic-update-slice_fusion), channel_id=1, source_target_pairs={{0,4},{4,8},{8,12},{12,16},{16,20},{20,24},{24,28},{28,0},{1,5},{5... | collective-permute-start | bytes 847880 | tf_op jit(solution)/shard_map/ppermute | solution.py:16
  13.2 3.1 %collective-permute-start.1 = (bf16[1,141312]{1,0:T(2,128)(2,1)S(1)}, bf16[1,141312]{1,0:T(2,128)(2,1)S(1)}, u32[]{:S(2)}, u32[]{:S(2)}) collective-permute-start(bf16[1,141312]{1,0:T(2,128)(2,1)S(1)} %constant_dynamic-update-slice_fusion), channel_id=1, source_target_pairs={{0,28},{4,0},{8,4},{12,8},{16,12},{20,16},{24,20},{28,24},{1,29},{... | collective-permute-start | bytes 847880 | tf_op jit(solution)/shard_map/ppermute | solution.py:19
  19.5 1.0 copy.45
  20.5 4.3 %all-to-all-start = ((bf16[2,8,64,512]{3,2,0,1:T(8,128)(2,1)}), bf16[2,8,64,512]{3,2,0,1:T(8,128)(2,1)}, u32[]{:S(2)}, u32[]{:S(2)}) async-start(bf16[2,8,64,512]{3,2,0,1:T(8,128)(2,1)} %copy.45), calls=%async_computation | async-start | bytes 2097152 | tf_op jit(solution)/shard_map/all_to_all | solution.py:146
  26.1 1.0 gather_fusion.4
  27.3 18.1 %collective-permute-done = bf16[1,141312]{1,0:T(2,128)(2,1)S(1)} collective-permute-done((bf16[1,141312]{1,0:T(2,128)(2,1)S(1)}, bf16[1,141312]{1,0:T(2,128)(2,1)S(1)}, u32[]{:S(2)}, u32[]{:S(2)}) %collective-permute-start) | collective-permute-done | bytes 282656 | tf_op jit(solution)/shard_map/ppermute | solution.py:16
  45.4 2.5 collective-permute-start.2
  48.3 1.0 gather_fusion.5
  49.6 11.9 %collective-permute-done.1 = bf16[1,141312]{1,0:T(2,128)(2,1)S(1)} collective-permute-done((bf16[1,141312]{1,0:T(2,128)(2,1)S(1)}, bf16[1,141312]{1,0:T(2,128)(2,1)S(1)}, u32[]{:S(2)}, u32[]{:S(2)}) %collective-permute-start.1) | collective-permute-done | bytes 282656 | tf_op jit(solution)/shard_map/ppermute | solution.py:19
  61.6 11.3 %collective-permute-done.2 = bf16[1,141312]{1,0:T(2,128)(2,1)S(1)} collective-permute-done((bf16[1,141312]{1,0:T(2,128)(2,1)S(1)}, bf16[1,141312]{1,0:T(2,128)(2,1)S(1)}, u32[]{:S(2)}, u32[]{:S(2)}) %collective-permute-start.2) | collective-permute-done | bytes 282656 | tf_op jit(solution)/shard_map/ppermute | solution.py:16
  72.8 2.5 collective-permute-start.4
  75.6 1.5 broadcast_in_dim.78
  77.1 11.3 %dynamic_update_slice.24 = bf16[8,141312]{1,0:T(8,128)(2,1)} dynamic-update-slice(bf16[8,141312]{1,0:T(8,128)(2,1)} %broadcast_in_dim.78, bf16[1,141312]{1,0:T(2,128)(2,1)S(1)} %constant_dynamic-update-slice_fusion, s32[]{:T(128)S(6)} %select_n.184, s32[]{:T(128)} %constant.152.clone.1) | dynamic-update-slice | bytes 565252 | tf_op jit(solution)/shard_map/dynamic_update_slice | solution.py:13
  88.6 3.1 %collective-permute-start.5 = (bf16[1,141312]{1,0:T(2,128)(2,1)}, bf16[1,141312]{1,0:T(2,128)(2,1)S(1)}, u32[]{:S(2)}, u32[]{:S(2)}) collective-permute-start(bf16[1,141312]{1,0:T(2,128)(2,1)} %collective-permute-done.3), channel_id=1, source_target_pairs={{0,28},{4,0},{8,4},{12,8},{16,12},{20,16},{24,20},{28,24},{1,29},{... | collective-permute-start | bytes 847880 | tf_op jit(solution)/shard_map/ppermute | solution.py:19
  91.7 11.3 %dynamic_update_slice.25 = bf16[8,141312]{1,0:T(8,128)(2,1)} dynamic-update-slice(bf16[8,141312]{1,0:T(8,128)(2,1)} %dynamic_update_slice.24, bf16[1,141312]{1,0:T(2,128)(2,1)S(1)} %collective-permute-done, s32[]{:T(128)S(6)} %select_n.199, s32[]{:T(128)} %constant.152.clone.1) | dynamic-update-slice | bytes 565252 | tf_op jit(solution)/shard_map/dynamic_update_slice | solution.py:17
  103.0 11.3 %dynamic_update_slice.26 = bf16[8,141312]{1,0:T(8,128)(2,1)} dynamic-update-slice(bf16[8,141312]{1,0:T(8,128)(2,1)} %dynamic_update_slice.25, bf16[1,141312]{1,0:T(2,128)(2,1)S(1)} %collective-permute-done.1, s32[]{:T(128)S(6)} %select_n.201, s32[]{:T(128)} %constant.152.clone.1) | dynamic-update-slice | bytes 565252 | tf_op jit(solution)/shard_map/dynamic_update_slice | solution.py:20
  114.3 11.3 %dynamic_update_slice.27 = bf16[8,141312]{1,0:T(8,128)(2,1)} dynamic-update-slice(bf16[8,141312]{1,0:T(8,128)(2,1)} %dynamic_update_slice.26, bf16[1,141312]{1,0:T(2,128)(2,1)S(1)} %collective-permute-done.2, s32[]{:T(128)S(6)} %select_n.203, s32[]{:T(128)} %constant.152.clone.1) | dynamic-update-slice | bytes 565252 | tf_op jit(solution)/shard_map/dynamic_update_slice | solution.py:17
  125.6 11.3 %dynamic_update_slice.28 = bf16[8,141312]{1,0:T(8,128)(2,1)} dynamic-update-slice(bf16[8,141312]{1,0:T(8,128)(2,1)} %dynamic_update_slice.27, bf16[1,141312]{1,0:T(2,128)(2,1)} %collective-permute-done.3, s32[]{:T(128)S(6)} %select_n.205, s32[]{:T(128)} %constant.152.clone.1) | dynamic-update-slice | bytes 565252 | tf_op jit(solution)/shard_map/dynamic_update_slice | solution.py:20
  136.9 11.3 %dynamic_update_slice.29 = bf16[8,141312]{1,0:T(8,128)(2,1)} dynamic-update-slice(bf16[8,141312]{1,0:T(8,128)(2,1)} %dynamic_update_slice.28, bf16[1,141312]{1,0:T(2,128)(2,1)} %collective-permute-done.4, s32[]{:T(128)S(6)} %select_n.207, s32[]{:T(128)} %constant.152.clone.1) | dynamic-update-slice | bytes 565252 | tf_op jit(solution)/shard_map/dynamic_update_slice | solution.py:17
  148.2 11.3 %dynamic_update_slice.30 = bf16[8,141312]{1,0:T(8,128)(2,1)} dynamic-update-slice(bf16[8,141312]{1,0:T(8,128)(2,1)} %dynamic_update_slice.29, bf16[1,141312]{1,0:T(2,128)(2,1)S(1)} %collective-permute-done.5, s32[]{:T(128)S(6)} %select_n.209, s32[]{:T(128)} %constant.152.clone.1) | dynamic-update-slice | bytes 565252 | tf_op jit(solution)/shard_map/dynamic_update_slice | solution.py:20
  159.5 11.3 %dynamic_update_slice.31 = bf16[8,141312]{1,0:T(8,128)(2,1)} dynamic-update-slice(bf16[8,141312]{1,0:T(8,128)(2,1)} %dynamic_update_slice.30, bf16[1,141312]{1,0:T(2,128)(2,1)S(1)} %collective-permute-done.6, s32[]{:T(128)S(6)} %select_n.211, s32[]{:T(128)} %constant.152.clone.1) | dynamic-update-slice | bytes 565252 | tf_op jit(solution)/shard_map/dynamic_update_slice | solution.py:17
  170.8 1.7 fusion.34
  172.6 1.3 gather_fusion.2
  173.9 2.3 gather_fusion.3
  176.2 1.3 copy.46
  178.1 1.0 bitcast_select_fusion
  179.4 4.5 %maximum_select_fusion = bf16[8,141312]{1,0:T(8,128)(2,1)S(1)} fusion(bf16[8,70656]{1,0:T(8,128)(2,1)} %gather_fusion.3, bf16[8,70656]{1,0:T(8,128)(2,1)S(1)} %gather_fusion.2, pred[8]{0:T(512)(128)(4,1)S(1)} %get-tuple-element.13), kind=kLoop, calls=%fused_computation.15 | loop fusion | flops 5652480 | bytes 4521992 | tf_op jit(solution)/shard_map/jit(_take)/select_n | solution.py:135
  184.0 1.3 copy-done
  185.3 5.0 %reshape.322 = bf16[8,2048,32]{2,1,0:T(8,128)(2,1)} reshape(bf16[8,65536]{1,0:T(8,128)(2,1)S(1)} %slice.44) | data formatting | bytes 2097152 | tf_op jit(solution)/shard_map/reshape | solution.py:44
  190.3 4.6 %copy.49 = bf16[8,2048,32]{1,2,0:T(8,128)(2,1)} copy(bf16[8,2048,32]{2,1,0:T(8,128)(2,1)} %reshape.322) | data formatting | bytes 2097152 | tf_op jit(solution)/shard_map/reshape | solution.py:44
  195.0 1.5 reshape.325
  196.5 0.9 copy.54
  197.4 5.9 %all-gather.2.cloned.1.call-done = bf16[512,2048]{1,0:T(8,128)(2,1)} async-done(((bf16[512,512]{1,0:T(8,128)(2,1)}), bf16[512,2048]{1,0:T(8,128)(2,1)}) %all-gather.2.cloned.1.call-update) | async-done | bytes 2097168 | tf_op jit(solution)/shard_map/all_gather | solution.py:159
  203.3 2.2 fusion
  205.6 2.1 fusion.27
  208.1 1.6 copy-done.10
  209.7 2.4 fusion.29
  212.1 2.4 fusion.25
  216.6 2.3 fusion.35
  218.9 3.5 %fusion.3 = bf16[512,2048]{1,0:T(8,128)(2,1)} fusion(f32[512,2048]{1,0:T(8,128)S(1)} %fusion.35, bf16[1,8,16,2048]{3,1,2,0:T(8,128)(2,1)S(1)} %bitcast.88, f32[512,8,16]{0,2,1:T(8,128)S(1)} %bitcast.101, f32[512,8]{0,1:T(8,128)S(1)} %fusion.19), kind=kOutput, calls=%fused_computation.13 | convolution fusion | flops 1612775424 | bytes 7094272 | tf_op jit(solution)/shard_map/tsr,srd->td/dot_general | solution.py:100
  222.4 31.6 %reduce-scatter.2.cloned.1.call-done = bf16[512,512]{1,0:T(8,128)(2,1)} async-done(((bf16[512,2048]{1,0:T(8,128)(2,1)}), bf16[512,512]{1,0:T(8,128)(2,1)}) %reduce-scatter.2.cloned.1.call-update) | async-done | bytes 524304 | tf_op jit(solution)/shard_map/reduce_scatter | solution.py:163
  254.1 1.8 scatter_fusion
  255.8 1.1 copy.55
  256.9 5.5 %all-to-all-start.1 = ((bf16[2,8,64,512]{3,2,0,1:T(8,128)(2,1)}), bf16[2,8,64,512]{3,2,0,1:T(8,128)(2,1)S(1)}, u32[]{:S(2)}, u32[]{:S(2)}) async-start(bf16[2,8,64,512]{3,2,0,1:T(8,128)(2,1)} %copy.55), calls=%async_computation.2 | async-start | bytes 2097152 | tf_op jit(solution)/shard_map/all_to_all | solution.py:171
  263.7 24.5 %all-to-all-done.1 = bf16[2,8,64,512]{3,2,0,1:T(8,128)(2,1)S(1)} async-done(((bf16[2,8,64,512]{3,2,0,1:T(8,128)(2,1)}), bf16[2,8,64,512]{3,2,0,1:T(8,128)(2,1)S(1)}, u32[]{:S(2)}, u32[]{:S(2)}) %all-to-all-start.1) | async-done | bytes 1048608 | tf_op jit(solution)/shard_map/all_to_all | solution.py:171
  288.7 1.4 fusion.4
  (95 shorter events, 10.4 us)
Async XLA Ops:
  6.5 2.8 copy-start.5
  6.5 3.2 %copy-start.4 = (bf16[1,16,2048]{2,1,0:T(8,128)(2,1)S(1)}, bf16[1,16,2048]{2,1,0:T(8,128)(2,1)}, u32[]{:S(2)}) copy-start(bf16[1,16,2048]{2,1,0:T(8,128)(2,1)} %param.24) | copy-start | bytes 196612
  6.5 9.7 %copy-start.6 = (s32[8,4]{0,1:T(4,128)S(1)}, s32[8,4]{0,1:T(4,128)}, u32[]{:S(2)}) copy-start(s32[8,4]{0,1:T(4,128)} %param.25) | copy-start | bytes 388
  6.5 12.5 %copy-start.1 = (bf16[1024,512]{1,0:T(8,128)(2,1)S(1)}, bf16[1024,512]{1,0:T(8,128)(2,1)}, u32[]{:S(2)}) copy-start(bf16[1024,512]{1,0:T(8,128)(2,1)} %param.16) | copy-start | bytes 3145732
  10.2 35.2 %collective-permute-start = (bf16[1,141312]{1,0:T(2,128)(2,1)S(1)}, bf16[1,141312]{1,0:T(2,128)(2,1)S(1)}, u32[]{:S(2)}, u32[]{:S(2)}) collective-permute-start(bf16[1,141312]{1,0:T(2,128)(2,1)S(1)} %constant_dynamic-update-slice_fusion), channel_id=1, source_target_pairs={{0,4},{4,8},{8,12},{12,16},{16,20},{20,24},{24,28},{28,0},{1,5},{5... | collective-permute-start | bytes 847880 | tf_op jit(solution)/shard_map/ppermute | solution.py:16
  13.2 48.4 %collective-permute-start.1 = (bf16[1,141312]{1,0:T(2,128)(2,1)S(1)}, bf16[1,141312]{1,0:T(2,128)(2,1)S(1)}, u32[]{:S(2)}, u32[]{:S(2)}) collective-permute-start(bf16[1,141312]{1,0:T(2,128)(2,1)S(1)} %constant_dynamic-update-slice_fusion), channel_id=1, source_target_pairs={{0,28},{4,0},{8,4},{12,8},{16,12},{20,16},{24,20},{28,24},{1,29},{... | collective-permute-start | bytes 847880 | tf_op jit(solution)/shard_map/ppermute | solution.py:19
  19.5 5.7 %copy-start.9 = (s32[8]{0:T(128)S(1)}, s32[8]{0:T(128)}, u32[]{:S(2)}) copy-start(s32[8]{0:T(128)} %param.27) | copy-start | bytes 100
  20.5 155.7 %all-to-all-start = ((bf16[2,8,64,512]{3,2,0,1:T(8,128)(2,1)}), bf16[2,8,64,512]{3,2,0,1:T(8,128)(2,1)}, u32[]{:S(2)}, u32[]{:S(2)}) async-start(bf16[2,8,64,512]{3,2,0,1:T(8,128)(2,1)} %copy.45), calls=%async_computation | async-start | bytes 2097152 | tf_op jit(solution)/shard_map/all_to_all | solution.py:146
  24.8 23.4 %copy-start.8 = (s32[8,4]{0,1:T(4,128)S(1)}, s32[8,4]{0,1:T(4,128)}, u32[]{:S(2)}) copy-start(s32[8,4]{0,1:T(4,128)} %param.26) | copy-start | bytes 388
  24.8 178.5 %all-gather.2.cloned.1.call-start = ((), (), s32[]{:S(2)}) async-start(), calls=%async_computation.3 | async-start | bytes 2621440 | tf_op jit(solution)/shard_map/all_gather | solution.py:159
  45.4 27.4 %collective-permute-start.2 = (bf16[1,141312]{1,0:T(2,128)(2,1)S(1)}, bf16[1,141312]{1,0:T(2,128)(2,1)S(1)}, u32[]{:S(2)}, u32[]{:S(2)}) collective-permute-start(bf16[1,141312]{1,0:T(2,128)(2,1)S(1)} %collective-permute-done), channel_id=1, source_target_pairs={{0,4},{4,8},{8,12},{12,16},{16,20},{20,24},{24,28},{28,0},{1,5},{5... | collective-permute-start | bytes 847880 | tf_op jit(solution)/shard_map/ppermute | solution.py:16
  49.6 38.9 %copy-start.7 = (bf16[2048]{0:T(1024)(128)(2,1)S(1)}, bf16[2048]{0:T(1024)(128)(2,1)}, u32[]{:S(2)}) copy-start(bf16[2048]{0:T(1024)(128)(2,1)} %param.17) | copy-start | bytes 12292
  61.5 27.0 %collective-permute-start.3 = (bf16[1,141312]{1,0:T(2,128)(2,1)S(1)}, bf16[1,141312]{1,0:T(2,128)(2,1)}, u32[]{:S(2)}, u32[]{:S(2)}) collective-permute-start(bf16[1,141312]{1,0:T(2,128)(2,1)S(1)} %collective-permute-done.1), channel_id=1, source_target_pairs={{0,28},{4,0},{8,4},{12,8},{16,12},{20,16},{24,20},{28,24},{1,29},{... | collective-permute-start | bytes 847880 | tf_op jit(solution)/shard_map/ppermute | solution.py:19
  72.8 18.9 %collective-permute-start.4 = (bf16[1,141312]{1,0:T(2,128)(2,1)S(1)}, bf16[1,141312]{1,0:T(2,128)(2,1)}, u32[]{:S(2)}, u32[]{:S(2)}) collective-permute-start(bf16[1,141312]{1,0:T(2,128)(2,1)S(1)} %collective-permute-done.2), channel_id=1, source_target_pairs={{0,4},{4,8},{8,12},{12,16},{16,20},{20,24},{24,28},{28,0},{1,5},{5... | collective-permute-start | bytes 847880 | tf_op jit(solution)/shard_map/ppermute | solution.py:16
  88.6 59.7 %collective-permute-start.5 = (bf16[1,141312]{1,0:T(2,128)(2,1)}, bf16[1,141312]{1,0:T(2,128)(2,1)S(1)}, u32[]{:S(2)}, u32[]{:S(2)}) collective-permute-start(bf16[1,141312]{1,0:T(2,128)(2,1)} %collective-permute-done.3), channel_id=1, source_target_pairs={{0,28},{4,0},{8,4},{12,8},{16,12},{20,16},{24,20},{28,24},{1,29},{... | collective-permute-start | bytes 847880 | tf_op jit(solution)/shard_map/ppermute | solution.py:19
  91.7 67.9 %collective-permute-start.6 = (bf16[1,141312]{1,0:T(2,128)(2,1)}, bf16[1,141312]{1,0:T(2,128)(2,1)S(1)}, u32[]{:S(2)}, u32[]{:S(2)}) collective-permute-start(bf16[1,141312]{1,0:T(2,128)(2,1)} %collective-permute-done.4), channel_id=1, source_target_pairs={{0,4},{4,8},{8,12},{12,16},{16,20},{20,24},{24,28},{28,0},{1,5},{5... | collective-permute-start | bytes 847880 | tf_op jit(solution)/shard_map/ppermute | solution.py:16
  179.1 74.8 %reduce-scatter.2.cloned.1.call-start = ((), (), s32[]{:S(2)}) async-start(), calls=%async_computation.4 | async-start | bytes 2621440 | tf_op jit(solution)/shard_map/reduce_scatter | solution.py:163
  183.9 1.4 copy-start
  190.3 4.6 %slice-start = ((bf16[8,141312]{1,0:T(8,128)(2,1)}), bf16[8,28672]{1,0:T(8,128)(2,1)S(1)}, s32[]{:S(2)}) async-start(bf16[8,141312]{1,0:T(8,128)(2,1)} %copy-done), calls=%async_computation.5 | async-start | bytes 917504 | tf_op jit(solution)/shard_map/slice | solution.py:47
  190.3 4.7 %slice-start.1 = ((bf16[8,141312]{1,0:T(8,128)(2,1)}), bf16[8,14336]{1,0:T(8,128)(2,1)S(1)}, s32[]{:S(2)}) async-start(bf16[8,141312]{1,0:T(8,128)(2,1)} %copy-done), calls=%async_computation.6 | async-start | bytes 458752 | tf_op jit(solution)/shard_map/slice | solution.py:50
  203.3 2.2 copy-start.3
  207.7 2.0 copy-start.10
  209.7 2.4 copy-start.11
  214.5 2.0 copy-start.12
  216.6 2.3 slice-start.2
  256.9 31.3 %all-to-all-start.1 = ((bf16[2,8,64,512]{3,2,0,1:T(8,128)(2,1)}), bf16[2,8,64,512]{3,2,0,1:T(8,128)(2,1)S(1)}, u32[]{:S(2)}, u32[]{:S(2)}) async-start(bf16[2,8,64,512]{3,2,0,1:T(8,128)(2,1)} %copy.55), calls=%async_computation.2 | async-start | bytes 2097152 | tf_op jit(solution)/shard_map/all_to_all | solution.py:171
  263.7 25.0 %copy-start.2 = (bf16[1024,512]{1,0:T(8,128)(2,1)S(1)}, bf16[1024,512]{1,0:T(8,128)(2,1)}, u32[]{:S(2)}) copy-start(bf16[1024,512]{1,0:T(8,128)(2,1)} %param.16) | copy-start | bytes 3145732
Sparse Core Ops, SparseCore 0:
  179.3 24.0 all-gather.1
  222.5 31.4 reduce-scatter.1
